TPU v7x, 32 devices: a whole 2x2x4 slice. The times are simulated.
32 devices in a mesh: row: 4 (over x, core), col: 4 (over z), pt: 2 (over y).
Axes of the slice: x: 2, y: 2, z: 4, core: 2. Of those that a mesh axis runs over, the one named last changes fastest.
Arguments:
- first_factors: int32 [32, 1024, 1024], P('pt', 'row', 'col'), may hold values from 0 to 12288
- second_factors: int32 [32, 1024, 1024], P('pt', 'row', 'col'), may hold values from 0 to 12288
Outputs:
- scaled_product: float32 [45, 1024, 1024], P(None, ('row', 'pt'), 'col')
All inputs are finite; a program needn't handle non-finite values.
Results may differ from a plain program's by a relative error of at most 0.0003.
Values may be sent and summed in bfloat16 or wider, within the bound.
A program may use at most 128 MiB of HBM per device.

v0:
```python
import jax
import jax.numpy as jnp
import numpy as np
from jax import lax
from jax.sharding import PartitionSpec as P

DEG = 16
modulus = 12289
digit_base = 128


def primitive_root():
    for candidate in range(2, modulus):
        if pow(candidate, 6144, modulus) != 1 and pow(candidate, 4096, modulus) != 1:
            return candidate
    return 0


def make_table(order_size, row_count, column_count, inverse):
    generator = primitive_root()
    root_value = pow(generator, (modulus - 1) // order_size, modulus)
    scaling = 1
    if inverse:
        root_value = pow(root_value, modulus - 2, modulus)
        scaling = pow(order_size, modulus - 2, modulus)
    entries = [
        [
            pow(root_value, row_index * column_index % order_size, modulus) * scaling % modulus
            for column_index in range(column_count)
        ]
        for row_index in range(row_count)
    ]
    return np.array(entries, dtype=np.int64)


def value_digits(values):
    high_digit = values // digit_base
    return (
        high_digit.astype(jnp.bfloat16),
        (values - digit_base * high_digit).astype(jnp.bfloat16),
    )


def combine(high_high, high_low, low_high, low_low):
    top_part = high_high.astype(jnp.int32) % modulus
    middle_part = (high_low.astype(jnp.int32) + low_high.astype(jnp.int32)) % modulus
    return (
        top_part * (digit_base * digit_base) % modulus
        + middle_part * digit_base
        + low_low.astype(jnp.int32)
    ) % modulus


def transform(matrix_table, coefs):
    slot_count = coefs.shape[0]
    flat_coefs = coefs.reshape(slot_count, -1)
    table_high = jnp.asarray(matrix_table // digit_base, dtype=jnp.bfloat16)
    table_low = jnp.asarray(matrix_table % digit_base, dtype=jnp.bfloat16)
    data_high, data_low = value_digits(flat_coefs)

    def product_of(left_part, right_part):
        return jnp.dot(left_part, right_part, preferred_element_type=jnp.float32)

    mixed_values = combine(
        product_of(table_high, data_high),
        product_of(table_high, data_low),
        product_of(table_low, data_high),
        product_of(table_low, data_low),
    )
    return mixed_values.reshape(matrix_table.shape[0], coefs.shape[1], coefs.shape[2])


def batched_product(left_part, right_part):
    return jnp.einsum("bik,bkj->bij", left_part, right_part, preferred_element_type=jnp.float32)


def digit_sum(totals, left_digits, right_digits):
    return (
        totals[0] + batched_product(left_digits[0], right_digits[0]),
        totals[1] + batched_product(left_digits[0], right_digits[1]),
        totals[2] + batched_product(left_digits[1], right_digits[0]),
        totals[3] + batched_product(left_digits[1], right_digits[1]),
    )


def pointwise(left_values, right_values):
    left_points, right_points = (
        lax.all_to_all(
            lax.all_to_all(
                left_values.astype(jnp.float32), "col", split_axis=0, concat_axis=2, tiled=True
            ),
            "pt",
            split_axis=0,
            concat_axis=1,
            tiled=True,
        ),
        lax.all_to_all(
            lax.all_to_all(
                right_values.astype(jnp.float32), "col", split_axis=0, concat_axis=2, tiled=True
            ),
            "pt",
            split_axis=0,
            concat_axis=1,
            tiled=True,
        ),
    )
    left_digits = value_digits(left_points.astype(jnp.int32))
    right_digits = value_digits(right_points.astype(jnp.int32))
    zeros_init = jnp.zeros(left_points.shape, jnp.float32)
    column_parts = tuple((digit_part for digit_part in left_digits))
    totals = digit_sum(
        (zeros_init, zeros_init, zeros_init, zeros_init),
        column_parts,
        (
            lax.all_gather(right_digits[0], "row", axis=1, tiled=True),
            lax.all_gather(right_digits[1], "row", axis=1, tiled=True),
        ),
    )
    product_values = combine(totals[0], totals[1], totals[2], totals[3]).astype(jnp.float32)
    arrived = lax.all_to_all(
        lax.all_to_all(product_values, "col", split_axis=2, concat_axis=0, tiled=True),
        "pt",
        split_axis=1,
        concat_axis=0,
        tiled=True,
    )
    col_count = lax.axis_size("col")
    pt_count = lax.axis_size("pt")
    local_count = arrived.shape[0] // (col_count * pt_count)
    returned = arrived.reshape(pt_count, col_count, local_count, arrived.shape[1], arrived.shape[2])
    returned = returned.transpose(1, 0, 2, 3, 4).reshape(arrived.shape)
    return returned.astype(jnp.int32)


def local(first_factors, second_factors):
    forward_one = make_table(2 * DEG, 2 * DEG, DEG, False)
    inverse_one = make_table(2 * DEG, 2 * DEG, 2 * DEG, True)
    forward_two = make_table(4 * DEG, 4 * DEG, 2 * DEG, False)
    inverse_two = make_table(4 * DEG, 3 * DEG - 3, 4 * DEG, True)
    first_entries, second_entries = (
        lax.all_to_all(
            first_factors.astype(jnp.float32), "pt", split_axis=1, concat_axis=0, tiled=True
        ),
        lax.all_to_all(
            second_factors.astype(jnp.float32), "pt", split_axis=1, concat_axis=0, tiled=True
        ),
    )
    first_entries = first_entries.astype(jnp.int32)
    second_entries = second_entries.astype(jnp.int32)
    left_values = jnp.concatenate(
        [transform(forward_one, first_entries[:DEG]), transform(forward_one, first_entries[DEG:])],
        0,
    )
    right_values = jnp.concatenate(
        [
            transform(forward_one, second_entries[:DEG]),
            transform(forward_one, second_entries[DEG:]),
        ],
        0,
    )
    products = pointwise(left_values, right_values)
    first_product = transform(inverse_one, products[: 2 * DEG])
    second_product = transform(inverse_one, products[2 * DEG :])
    upper_values = transform(forward_two, first_product)
    lower_values = transform(forward_two[:, :DEG], second_product[DEG:])
    result_coefficients = transform(inverse_two, pointwise(upper_values, lower_values))
    return result_coefficients.astype(jnp.float32) / 12289.0


def reduce_centred(values):
    return values - 12289.0 * jnp.round(values * (1.0 / 12289.0))


def centred_digits(values):
    high_digit = jnp.round(values * (1.0 / 128.0))
    return (high_digit.astype(jnp.bfloat16), (values - 128.0 * high_digit).astype(jnp.bfloat16))


def combine_centred(high_high, middle, low_low):
    upper_part = reduce_centred(reduce_centred(high_high) * 128.0 + middle)
    return reduce_centred(upper_part * 128.0 + low_low)


def table_digits(matrix_table):
    centred = np.where(matrix_table > modulus // 2, matrix_table - modulus, matrix_table)
    high_digit = np.round(centred / 128.0)
    return (high_digit, centred - 128.0 * high_digit)


def centred_transform(table_high, table_low, coefs):
    data_high, data_low = centred_digits(coefs.astype(jnp.float32))
    table_high = jnp.asarray(table_high, dtype=jnp.bfloat16)
    table_low = jnp.asarray(table_low, dtype=jnp.bfloat16)

    def product_of(left_part, right_part):
        return jnp.einsum("ts,sab->tab", left_part, right_part, preferred_element_type=jnp.float32)

    middle = product_of(
        jnp.concatenate([table_high, table_low], 1), jnp.concatenate([data_low, data_high], 0)
    )
    return combine_centred(
        product_of(table_high, data_high), middle, product_of(table_low, data_low)
    )


def column_pointwise(left_values, right_values):
    right_points = lax.all_to_all(
        right_values.astype(jnp.int16), "col", split_axis=0, concat_axis=2, tiled=True
    )
    right_points = lax.all_gather(right_points, "row", axis=1, tiled=True)
    left_points = lax.all_to_all(
        left_values.astype(jnp.int16), "col", split_axis=0, concat_axis=2, tiled=True
    )
    left_high, left_low = centred_digits(left_points.astype(jnp.float32))
    right_high, right_low = centred_digits(right_points.astype(jnp.float32))
    middle = batched_product(left_high, right_low) + batched_product(left_low, right_high)
    product_values = combine_centred(
        batched_product(left_high, right_high), middle, batched_product(left_low, right_low)
    )
    return lax.all_to_all(
        product_values.astype(jnp.int16), "col", split_axis=2, concat_axis=0, tiled=True
    )


def pair_local(first_factors, second_factors):
    forward_one = table_digits(make_table(2 * DEG, 2 * DEG, DEG, False))
    inverse_one = table_digits(make_table(2 * DEG, 2 * DEG, 2 * DEG, True))
    forward_two = table_digits(make_table(4 * DEG, 4 * DEG, 2 * DEG, False))
    inverse_two = table_digits(make_table(4 * DEG, 3 * DEG - 3, 4 * DEG, True))
    half_points = 2 * DEG
    place = lax.axis_index("pt")
    products = column_pointwise(
        centred_transform(*forward_one, centre(first_factors)),
        centred_transform(*forward_one, centre(second_factors)),
    )
    own_product = centred_transform(*inverse_one, products).astype(jnp.int16)
    both_products = lax.all_gather(own_product, "pt", axis=0, tiled=True)
    first_product = both_products[: 2 * DEG]
    shifted = both_products[3 * DEG :]
    own_tables = [
        lax.dynamic_slice_in_dim(
            jnp.asarray(digit, dtype=jnp.bfloat16), place * half_points, half_points, 0
        )
        for digit in forward_two
    ]
    upper_values = centred_transform(*own_tables, first_product)
    lower_values = centred_transform(*[digit[:, :DEG] for digit in own_tables], shifted)
    products_two = column_pointwise(upper_values, lower_values)
    all_points = lax.all_to_all(products_two, "pt", split_axis=1, concat_axis=0, tiled=True)
    result = centred_transform(*inverse_two, all_points)
    return jnp.where(result < 0.0, result + 12289.0, result) / 12289.0


def centre(values):
    return jnp.where(values > modulus // 2, values - modulus, values)


def solution(mesh):
    in_specs = (P("pt", "row", "col"), P("pt", "row", "col"))
    out_specs = P(None, ("row", "pt"), "col")
    body = pair_local if mesh.shape["pt"] == 2 else local
    return jax.shard_map(body, mesh=mesh, in_specs=in_specs, out_specs=out_specs, check_vma=False)
```

profile of v0, /device:TPU:0, one launch (start us, length us, event | category | flops | bytes accessed | tf_op | source)
XLA Modules:
  0.0 1258.8 jit_solution(4259190581243966023)
XLA Ops:
  45.8 73.8 %all-to-all-done = s16[32,256,256]{2,1,0:T(8,128)(2,1)} async-done(((s16[32,256,256]{2,1,0:T(8,128)(2,1)}), s16[32,256,256]{2,1,0:T(8,128)(2,1)}, u32[]{:S(2)}, u32[]{:S(2)}) %all-to-all-start) | async-done | bytes 4194336 | tf_op jit(solution)/shard_map/all_to_all | solution.py:211
  131.8 12.0 copy.111
  143.8 10.8 reshape.16
  154.6 63.0 %all-to-all-done.1 = s16[32,256,256]{2,1,0:T(8,128)(2,1)} async-done(((s16[32,256,256]{2,1,0:T(8,128)(2,1)}), s16[32,256,256]{2,1,0:T(8,128)(2,1)}, u32[]{:S(2)}, u32[]{:S(2)}) %all-to-all-start.1) | async-done | bytes 4194336 | tf_op jit(solution)/shard_map/all_to_all | solution.py:207
  217.6 7.4 copy.113
  225.0 7.9 all_to_all.71
  232.9 105.4 %all-gather.3 = s16[8,1024,1024]{2,1,0:T(8,128)(2,1)} all-gather(s16[8,256,1024]{2,1,0:T(8,128)(2,1)} %all_to_all.71), channel_id=1, replica_groups=mesh['row'=4,'col'=4,'pt'=2] {'row'}, dimensions={1}, use_global_device_ids=true | all-gather | bytes 20971520 | tf_op jit(solution)/shard_map/all_gather | solution.py:210
  338.4 16.5 %fusion.14 = f32[8,256,1024]{2,1,0:T(8,128)} fusion(s16[8,1024,1024]{2,1,0:T(8,128)(2,1)} %all-gather.3, f32[8,256,1024]{2,1,0:T(8,128)} %reshape.16), kind=kOutput, calls=%fused_computation.16 | convolution fusion | flops 4334813184 | bytes 33554432 | tf_op jit(solution)/shard_map/bik,bkj->bij/dot_general | solution.py:74
  354.9 17.6 %fusion.12 = f32[8,256,1024]{2,1,0:T(8,128)} fusion(s16[8,1024,1024]{2,1,0:T(8,128)(2,1)} %all-gather.3, f32[8,256,1024]{2,1,0:T(8,128)} %reshape.16), kind=kOutput, calls=%fused_computation.15 | convolution fusion | flops 4339007488 | bytes 33554432 | tf_op jit(solution)/shard_map/bik,bkj->bij/dot_general | solution.py:74
  372.5 18.3 %fusion.20 = f32[8,256,1024]{2,1,0:T(8,128)} fusion(s16[8,1024,1024]{2,1,0:T(8,128)(2,1)} %all-gather.3, f32[8,256,1024]{2,1,0:T(8,128)} %reshape.16), kind=kOutput, calls=%fused_computation.23 | convolution fusion | flops 4355784704 | bytes 33554432 | tf_op jit(solution)/shard_map/bik,bkj->bij/dot_general | solution.py:74
  390.8 25.6 %subtract_convert_fusion.5 = s16[8,256,1024]{2,1,0:T(8,128)(2,1)} fusion(f32[8,256,1024]{2,1,0:T(8,128)} %fusion.20, f32[8,256,1024]{2,1,0:T(8,128)} %fusion.12, f32[8,256,1024]{2,1,0:T(8,128)} %fusion.14, s16[8,1024,1024]{2,1,0:T(8,128)(2,1)} %all-gather.3, f32[8,256,1024]{2,1,0:T(8,128)} %reshape.16), kind=kOutput, calls=%fused_computation.59 | convolution fusion | flops 4389339136 | bytes 54525952 | tf_op jit(solution)/shard_map/bik,bkj->bij/dot_general | solution.py:74
  416.3 7.3 copy.76
  428.8 94.0 %all-to-all-done.2 = s16[8,256,1024]{1,0,2:T(8,128)(2,1)} async-done(((s16[8,256,1024]{1,0,2:T(8,128)(2,1)}), s16[8,256,1024]{1,0,2:T(8,128)(2,1)}, u32[]{:S(2)}, u32[]{:S(2)}) %all-to-all-start.2) | async-done | bytes 4194336 | tf_op jit(solution)/shard_map/all_to_all | solution.py:220
  529.3 10.5 copy.77
  547.0 8.1 subtract_convert_fusion.4
  555.1 92.8 %all-gather.4 = s16[64,256,256]{2,0,1:T(8,128)(2,1)S(1)} all-gather(s16[32,256,256]{2,0,1:T(8,128)(2,1)} %subtract_convert_fusion.4), channel_id=1, replica_groups=mesh['row'=4,'col'=4,'pt'=2] {'pt'}, dimensions={0}, use_global_device_ids=true | all-gather | bytes 12582912 | tf_op jit(solution)/shard_map/all_gather | solution.py:237
  657.1 10.0 subtract_convert_fusion.3
  682.9 8.5 subtract_convert_fusion.2
  698.0 70.7 %all-to-all-done.3 = s16[32,256,256]{2,1,0:T(8,128)(2,1)} async-done(((s16[32,256,256]{2,1,0:T(8,128)(2,1)}), s16[32,256,256]{2,1,0:T(8,128)(2,1)}, u32[]{:S(2)}, u32[]{:S(2)}) %all-to-all-start.3) | async-done | bytes 4194336 | tf_op jit(solution)/shard_map/all_to_all | solution.py:211
  780.6 12.0 copy.110
  792.6 10.8 reshape.18
  803.4 63.1 %all-to-all-done.4 = s16[32,256,256]{2,1,0:T(8,128)(2,1)} async-done(((s16[32,256,256]{2,1,0:T(8,128)(2,1)}), s16[32,256,256]{2,1,0:T(8,128)(2,1)}, u32[]{:S(2)}, u32[]{:S(2)}) %all-to-all-start.4) | async-done | bytes 4194336 | tf_op jit(solution)/shard_map/all_to_all | solution.py:207
  866.5 7.4 copy.112
  874.0 7.9 all_to_all.77
  881.9 104.5 %all-gather.5 = s16[8,1024,1024]{2,1,0:T(8,128)(2,1)} all-gather(s16[8,256,1024]{2,1,0:T(8,128)(2,1)} %all_to_all.77), channel_id=1, replica_groups=mesh['row'=4,'col'=4,'pt'=2] {'row'}, dimensions={1}, use_global_device_ids=true | all-gather | bytes 20971520 | tf_op jit(solution)/shard_map/all_gather | solution.py:210
  986.4 16.5 %fusion.10 = f32[8,256,1024]{2,1,0:T(8,128)} fusion(s16[8,1024,1024]{2,1,0:T(8,128)(2,1)} %all-gather.5, f32[8,256,1024]{2,1,0:T(8,128)} %reshape.18), kind=kOutput, calls=%fused_computation.14 | convolution fusion | flops 4334813184 | bytes 33554432 | tf_op jit(solution)/shard_map/bik,bkj->bij/dot_general | solution.py:74
  1002.9 17.6 %fusion.8 = f32[8,256,1024]{2,1,0:T(8,128)} fusion(s16[8,1024,1024]{2,1,0:T(8,128)(2,1)} %all-gather.5, f32[8,256,1024]{2,1,0:T(8,128)} %reshape.18), kind=kOutput, calls=%fused_computation.13 | convolution fusion | flops 4339007488 | bytes 33554432 | tf_op jit(solution)/shard_map/bik,bkj->bij/dot_general | solution.py:74
  1020.5 18.3 %fusion.16 = f32[8,256,1024]{2,1,0:T(8,128)} fusion(s16[8,1024,1024]{2,1,0:T(8,128)(2,1)} %all-gather.5, f32[8,256,1024]{2,1,0:T(8,128)} %reshape.18), kind=kOutput, calls=%fused_computation.21 | convolution fusion | flops 4355784704 | bytes 33554432 | tf_op jit(solution)/shard_map/bik,bkj->bij/dot_general | solution.py:74
  1038.7 25.6 %subtract_convert_fusion = s16[8,256,1024]{2,1,0:T(8,128)(2,1)} fusion(f32[8,256,1024]{2,1,0:T(8,128)} %fusion.16, f32[8,256,1024]{2,1,0:T(8,128)} %fusion.8, f32[8,256,1024]{2,1,0:T(8,128)} %fusion.10, s16[8,1024,1024]{2,1,0:T(8,128)(2,1)} %all-gather.5, f32[8,256,1024]{2,1,0:T(8,128)} %reshape.18), kind=kOutput, calls=%fused_computation.52 | convolution fusion | flops 4389339136 | bytes 54525952 | tf_op jit(solution)/shard_map/bik,bkj->bij/dot_general | solution.py:74
  1071.5 99.7 %all_to_all.90 = s16[8,256,1024]{1,0,2:T(8,128)(2,1)} all-to-all(s16[8,256,1024]{1,0,2:T(8,128)(2,1)} %copy.84), channel_id=1, replica_groups=mesh['row'=4,'col'=4,'pt'=2] {'col'}, dimensions={2} | all-to-all | bytes 8388608 | tf_op jit(solution)/shard_map/all_to_all | solution.py:220
  1171.2 7.9 copy.86
  1183.6 50.0 %all_to_all.91 = s16[32,256,256]{2,0,1:T(8,128)(2,1)S(1)} all-to-all(s16[32,256,256]{2,0,1:T(8,128)(2,1)S(1)} %copy.87), channel_id=1, replica_groups=mesh['row'=4,'col'=4,'pt'=2] {'pt'}, dimensions={1} | all-to-all | bytes 8388608 | tf_op jit(solution)/shard_map/all_to_all | solution.py:249
  (70 shorter events, 156.6 us)
Async XLA Ops:
  0.0 5.5 copy-start.3
  0.0 6.8 copy-start.2
  6.7 1.4 copy-start.11
  19.6 100.0 %all-to-all-start = ((s16[32,256,256]{2,1,0:T(8,128)(2,1)}), s16[32,256,256]{2,1,0:T(8,128)(2,1)}, u32[]{:S(2)}, u32[]{:S(2)}) async-start(s16[32,256,256]{2,1,0:T(8,128)(2,1)} %copy.69), calls=%async_computation | async-start | bytes 8388608 | tf_op jit(solution)/shard_map/all_to_all | solution.py:211
  119.6 98.0 %all-to-all-start.1 = ((s16[32,256,256]{2,1,0:T(8,128)(2,1)}), s16[32,256,256]{2,1,0:T(8,128)(2,1)}, u32[]{:S(2)}, u32[]{:S(2)}) async-start(s16[32,256,256]{2,1,0:T(8,128)(2,1)} %copy.74), calls=%async_computation.1 | async-start | bytes 8388608 | tf_op jit(solution)/shard_map/all_to_all | solution.py:207
  416.3 12.5 copy-start.1
  416.3 12.5 copy-start.4
  423.6 99.2 %all-to-all-start.2 = ((s16[8,256,1024]{1,0,2:T(8,128)(2,1)}), s16[8,256,1024]{1,0,2:T(8,128)(2,1)}, u32[]{:S(2)}, u32[]{:S(2)}) async-start(s16[8,256,1024]{1,0,2:T(8,128)(2,1)} %copy.76), calls=%async_computation.2 | async-start | bytes 8388608 | tf_op jit(solution)/shard_map/all_to_all | solution.py:220
  539.8 4.5 copy-start.8
  544.3 1.3 copy-start.7
  545.5 1.5 copy-start.10
  648.0 9.1 copy-start
  671.3 97.4 %all-to-all-start.3 = ((s16[32,256,256]{2,1,0:T(8,128)(2,1)}), s16[32,256,256]{2,1,0:T(8,128)(2,1)}, u32[]{:S(2)}, u32[]{:S(2)}) async-start(s16[32,256,256]{2,1,0:T(8,128)(2,1)} %copy.78), calls=%async_computation.3 | async-start | bytes 8388608 | tf_op jit(solution)/shard_map/all_to_all | solution.py:211
  676.4 4.3 slice-start
  679.4 2.2 slice-start.1
  768.7 97.8 %all-to-all-start.4 = ((s16[32,256,256]{2,1,0:T(8,128)(2,1)}), s16[32,256,256]{2,1,0:T(8,128)(2,1)}, u32[]{:S(2)}, u32[]{:S(2)}) async-start(s16[32,256,256]{2,1,0:T(8,128)(2,1)} %copy.82), calls=%async_computation.4 | async-start | bytes 8388608 | tf_op jit(solution)/shard_map/all_to_all | solution.py:207
  1242.3 2.2 copy-start.5
  1244.4 1.0 copy-start.6
  1245.4 1.5 copy-start.9
where the time goes:
time: 1270 us; the launch traced here: 1260 us
  blocking collectives  452 us (36%)
  waiting for transfers between devices  364 us (29%)
  matrix products  221 us (17%)
  local copies, waits for them, and re-layouts  148 us (12%)
  other arithmetic  45.2 us (4%)
  starting transfers between devices  27.2 us (2%)
    all_gather x2, blocking collectives, column_pointwise(): right_points = lax.all_gather(right_points, 'row', axis=1, tiled=True)  210 us
    dot_general x8, matrix products, batched_product(): jnp.einsum('bik,bkj->bij', left_part, right_part, preferred_element_type=...  156 us
    all_to_all x2, waiting for transfers between devices, column_pointwise(): lax.all_to_all(left_values.astype(jnp.int16), 'col', split_axis=0, concat...  144 us
    all_to_all x2, waiting for transfers between devices, column_pointwise(): lax.all_to_all(right_values.astype(jnp.int16), 'col', split_axis=0, conca...  126 us
    all_to_all x1, blocking collectives, column_pointwise(): lax.all_to_all(product_values.astype(jnp.int16), 'col', split_axis=2, con...  99.7 us
    all_to_all x1, waiting for transfers between devices, column_pointwise(): lax.all_to_all(product_values.astype(jnp.int16), 'col', split_axis=2, con...  94 us
    all_gather x1, blocking collectives, pair_local(): both_products = lax.all_gather(own_product, 'pt', axis=0, tiled=True)  92.8 us
    dot_general x18, matrix products, product_of(): jnp.einsum('ts,sab->tab', left_part, right_part, preferred_element_type=j...  65.3 us
  transfers between devices with their start and end apart: 5, of which 5 were waited for; matrix products, arithmetic and copies ran while one was open for 8% of the time, Pallas kernels for 0%

commit v1 on v0

--- a/solution.py
+++ b/solution.py
@@ -204,8 +204,14 @@
 
 
 def column_pointwise(left_values, right_values):
-    right_points = lax.all_to_all(
-        right_values.astype(jnp.int16), "col", split_axis=0, concat_axis=2, tiled=True
+    right_points = jnp.concatenate(
+        lax.all_to_all(
+            jnp.stack(jnp.split(right_values.astype(jnp.int16), lax.axis_size("col"), axis=0)),
+            "col",
+            0,
+            0,
+        ),
+        axis=2,
     )
     right_points = lax.all_gather(right_points, "row", axis=1, tiled=True)
     left_points = lax.all_to_all(

time: 1270 us -> 1200 us (0.945)
  waiting for transfers between devices: 364 us -> 303 us
    all_to_all x2, waiting for transfers between devices: 144 us -> 72.6 us  [column_pointwise(): lax.all_to_all(left_values.astype(jnp.int16), 'col', split_axis=0, concat...]
    all_to_all x4 -> x0, local copies, waits for them, and re-layouts: 30.7 us -> none  [column_pointwise(): lax.all_to_all(right_values.astype(jnp.int16), 'col', split_axis=0, conca...]
    reshape x0 -> x4, local copies, waits for them, and re-layouts: none -> 29.5 us  [column_pointwise(): jnp.concatenate(lax.all_to_all(jnp.stack(jnp.split(right_values.astype(jn...]
  transfers between devices with their start and end apart: 5 -> 5, of which waited for: 5 -> 4; matrix products, arithmetic and copies ran while one was open for 8% -> 7% of each run, Pallas kernels for 0% -> 0%
where the time goes in v1:
time: 1200 us; the launch traced here: 1190 us
  blocking collectives  452 us (38%)
  waiting for transfers between devices  303 us (25%)
  matrix products  221 us (18%)
  local copies, waits for them, and re-layouts  138 us (12%)
  other arithmetic  49.2 us (4%)
  starting transfers between devices  27.4 us (2%)
    all_gather x2, blocking collectives, column_pointwise(): right_points = lax.all_gather(right_points, 'row', axis=1, tiled=True)  210 us
    dot_general x8, matrix products, batched_product(): jnp.einsum('bik,bkj->bij', left_part, right_part, preferred_element_type=...  156 us
    all_to_all x2, waiting for transfers between devices, column_pointwise(): lax.all_to_all(jnp.stack(jnp.split(right_values.astype(jnp.int16), lax.ax...  137 us
    all_to_all x1, blocking collectives, column_pointwise(): lax.all_to_all(product_values.astype(jnp.int16), 'col', split_axis=2, con...  99.6 us
    all_to_all x1, waiting for transfers between devices, column_pointwise(): lax.all_to_all(product_values.astype(jnp.int16), 'col', split_axis=2, con...  94 us
    all_gather x1, blocking collectives, pair_local(): both_products = lax.all_gather(own_product, 'pt', axis=0, tiled=True)  92.9 us
    all_to_all x2, waiting for transfers between devices, column_pointwise(): lax.all_to_all(left_values.astype(jnp.int16), 'col', split_axis=0, concat...  72.6 us
    dot_general x18, matrix products, product_of(): jnp.einsum('ts,sab->tab', left_part, right_part, preferred_element_type=j...  65.3 us
  transfers between devices with their start and end apart: 5, of which 4 were waited for; matrix products, arithmetic and copies ran while one was open for 7% of the time, Pallas kernels for 0%

profile of v1, /device:TPU:0, one launch (start us, length us, event | category | flops | bytes accessed | tf_op | source)
XLA Modules:
  0.0 1192.9 jit_solution(9691909683596180064)
XLA Ops:
  8.2 7.1 subtract_convert_fusion.7
  32.8 7.1 subtract_convert_fusion.8
  44.2 73.8 %all-to-all-done.1 = s16[4,8,256,256]{3,1,2,0:T(8,128)(2,1)} async-done(((s16[4,8,256,256]{3,1,2,0:T(8,128)(2,1)}), s16[4,8,256,256]{3,1,2,0:T(8,128)(2,1)}, u32[]{:S(2)}, u32[]{:S(2)}) %all-to-all-start.1) | async-done | bytes 4194336 | tf_op jit(solution)/shard_map/all_to_all | solution.py:208
  122.9 7.9 copy.74
  137.7 105.3 %all-gather.3 = s16[8,1024,1024]{2,1,0:T(8,128)(2,1)} all-gather(s16[8,256,1024]{2,1,0:T(8,128)(2,1)} %copy.75), channel_id=1, replica_groups=mesh['row'=4,'col'=4,'pt'=2] {'row'}, dimensions={1}, use_global_device_ids=true | all-gather | bytes 20971520 | tf_op jit(solution)/shard_map/all_gather | solution.py:216
  249.8 12.0 %copy.109 = f32[4,8,256,256]{3,0,2,1:T(4,128)} copy(f32[4,8,256,256]{3,2,1,0:T(8,128)} %convert.12) | data formatting | bytes 16777216 | tf_op jit(solution)/shard_map/convert_element_type | solution.py:220
  261.8 10.8 reshape.32
  272.6 16.7 %fusion.14 = f32[8,256,1024]{2,1,0:T(8,128)} fusion(s16[8,1024,1024]{2,1,0:T(8,128)(2,1)} %all-gather.3, f32[8,256,1024]{2,1,0:T(8,128)} %reshape.32), kind=kOutput, calls=%fused_computation.16 | convolution fusion | flops 4334813184 | bytes 33554432 | tf_op jit(solution)/shard_map/bik,bkj->bij/dot_general | solution.py:74
  289.3 17.6 %fusion.12 = f32[8,256,1024]{2,1,0:T(8,128)} fusion(s16[8,1024,1024]{2,1,0:T(8,128)(2,1)} %all-gather.3, f32[8,256,1024]{2,1,0:T(8,128)} %reshape.32), kind=kOutput, calls=%fused_computation.15 | convolution fusion | flops 4339007488 | bytes 33554432 | tf_op jit(solution)/shard_map/bik,bkj->bij/dot_general | solution.py:74
  306.9 18.3 %fusion.20 = f32[8,256,1024]{2,1,0:T(8,128)} fusion(s16[8,1024,1024]{2,1,0:T(8,128)(2,1)} %all-gather.3, f32[8,256,1024]{2,1,0:T(8,128)} %reshape.32), kind=kOutput, calls=%fused_computation.23 | convolution fusion | flops 4355784704 | bytes 33554432 | tf_op jit(solution)/shard_map/bik,bkj->bij/dot_general | solution.py:74
  325.2 25.6 %subtract_convert_fusion.5 = s16[8,256,1024]{2,1,0:T(8,128)(2,1)} fusion(f32[8,256,1024]{2,1,0:T(8,128)} %fusion.20, f32[8,256,1024]{2,1,0:T(8,128)} %fusion.12, f32[8,256,1024]{2,1,0:T(8,128)} %fusion.14, s16[8,1024,1024]{2,1,0:T(8,128)(2,1)} %all-gather.3, f32[8,256,1024]{2,1,0:T(8,128)} %reshape.32), kind=kOutput, calls=%fused_computation.59 | convolution fusion | flops 4389339136 | bytes 54525952 | tf_op jit(solution)/shard_map/bik,bkj->bij/dot_general | solution.py:74
  350.8 7.3 copy.76
  363.5 94.0 %all-to-all-done.2 = s16[8,256,1024]{1,0,2:T(8,128)(2,1)} async-done(((s16[8,256,1024]{1,0,2:T(8,128)(2,1)}), s16[8,256,1024]{1,0,2:T(8,128)(2,1)}, u32[]{:S(2)}, u32[]{:S(2)}) %all-to-all-start.2) | async-done | bytes 4194336 | tf_op jit(solution)/shard_map/all_to_all | solution.py:226
  464.0 10.5 copy.77
  481.8 8.1 subtract_convert_fusion.4
  489.8 92.9 %all-gather.4 = s16[64,256,256]{2,0,1:T(8,128)(2,1)S(1)} all-gather(s16[32,256,256]{2,0,1:T(8,128)(2,1)} %subtract_convert_fusion.4), channel_id=1, replica_groups=mesh['row'=4,'col'=4,'pt'=2] {'pt'}, dimensions={0}, use_global_device_ids=true | all-gather | bytes 12582912 | tf_op jit(solution)/shard_map/all_gather | solution.py:243
  591.5 10.0 subtract_convert_fusion.3
  617.4 8.5 subtract_convert_fusion.2
  630.6 72.6 %all-to-all-done.3 = s16[32,256,256]{2,1,0:T(8,128)(2,1)} async-done(((s16[32,256,256]{2,1,0:T(8,128)(2,1)}), s16[32,256,256]{2,1,0:T(8,128)(2,1)}, u32[]{:S(2)}, u32[]{:S(2)}) %all-to-all-start.3) | async-done | bytes 4194336 | tf_op jit(solution)/shard_map/all_to_all | solution.py:217
  715.2 12.0 %copy.108 = f32[4,8,256,256]{3,0,2,1:T(4,128)} copy(f32[4,8,256,256]{3,2,1,0:T(8,128)} %convert.14) | data formatting | bytes 16777216 | tf_op jit(solution)/shard_map/convert_element_type | solution.py:220
  727.2 10.8 reshape.34
  738.0 63.1 %all-to-all-done.4 = s16[4,8,256,256]{3,1,2,0:T(8,128)(2,1)} async-done(((s16[4,8,256,256]{3,1,2,0:T(8,128)(2,1)}), s16[4,8,256,256]{3,1,2,0:T(8,128)(2,1)}, u32[]{:S(2)}, u32[]{:S(2)}) %all-to-all-start.4) | async-done | bytes 4194336 | tf_op jit(solution)/shard_map/all_to_all | solution.py:208
  801.1 7.9 copy.82
  815.9 104.5 %all-gather.5 = s16[8,1024,1024]{2,1,0:T(8,128)(2,1)} all-gather(s16[8,256,1024]{2,1,0:T(8,128)(2,1)} %copy.83), channel_id=1, replica_groups=mesh['row'=4,'col'=4,'pt'=2] {'row'}, dimensions={1}, use_global_device_ids=true | all-gather | bytes 20971520 | tf_op jit(solution)/shard_map/all_gather | solution.py:216
  920.4 16.5 %fusion.10 = f32[8,256,1024]{2,1,0:T(8,128)} fusion(s16[8,1024,1024]{2,1,0:T(8,128)(2,1)} %all-gather.5, f32[8,256,1024]{2,1,0:T(8,128)} %reshape.34), kind=kOutput, calls=%fused_computation.14 | convolution fusion | flops 4334813184 | bytes 33554432 | tf_op jit(solution)/shard_map/bik,bkj->bij/dot_general | solution.py:74
  936.9 17.6 %fusion.8 = f32[8,256,1024]{2,1,0:T(8,128)} fusion(s16[8,1024,1024]{2,1,0:T(8,128)(2,1)} %all-gather.5, f32[8,256,1024]{2,1,0:T(8,128)} %reshape.34), kind=kOutput, calls=%fused_computation.13 | convolution fusion | flops 4339007488 | bytes 33554432 | tf_op jit(solution)/shard_map/bik,bkj->bij/dot_general | solution.py:74
  954.5 18.2 %fusion.16 = f32[8,256,1024]{2,1,0:T(8,128)} fusion(s16[8,1024,1024]{2,1,0:T(8,128)(2,1)} %all-gather.5, f32[8,256,1024]{2,1,0:T(8,128)} %reshape.34), kind=kOutput, calls=%fused_computation.21 | convolution fusion | flops 4355784704 | bytes 33554432 | tf_op jit(solution)/shard_map/bik,bkj->bij/dot_general | solution.py:74
  972.8 25.6 %subtract_convert_fusion = s16[8,256,1024]{2,1,0:T(8,128)(2,1)} fusion(f32[8,256,1024]{2,1,0:T(8,128)} %fusion.16, f32[8,256,1024]{2,1,0:T(8,128)} %fusion.8, f32[8,256,1024]{2,1,0:T(8,128)} %fusion.10, s16[8,1024,1024]{2,1,0:T(8,128)(2,1)} %all-gather.5, f32[8,256,1024]{2,1,0:T(8,128)} %reshape.34), kind=kOutput, calls=%fused_computation.52 | convolution fusion | flops 4389339136 | bytes 54525952 | tf_op jit(solution)/shard_map/bik,bkj->bij/dot_general | solution.py:74
  998.3 7.3 copy.84
  1005.6 99.6 %all_to_all.64 = s16[8,256,1024]{1,0,2:T(8,128)(2,1)} all-to-all(s16[8,256,1024]{1,0,2:T(8,128)(2,1)} %copy.84), channel_id=1, replica_groups=mesh['row'=4,'col'=4,'pt'=2] {'col'}, dimensions={2} | all-to-all | bytes 8388608 | tf_op jit(solution)/shard_map/all_to_all | solution.py:226
  1105.3 7.9 copy.86
  1117.7 50.0 %all_to_all.65 = s16[32,256,256]{2,0,1:T(8,128)(2,1)S(1)} all-to-all(s16[32,256,256]{2,0,1:T(8,128)(2,1)S(1)} %copy.87), channel_id=1, replica_groups=mesh['row'=4,'col'=4,'pt'=2] {'pt'}, dimensions={1} | all-to-all | bytes 8388608 | tf_op jit(solution)/shard_map/all_to_all | solution.py:255
  (72 shorter events, 145.0 us)
Async XLA Ops:
  0.0 5.5 copy-start.3
  0.0 6.8 copy-start.2
  6.8 1.4 copy-start.11
  17.7 100.3 %all-to-all-start.1 = ((s16[4,8,256,256]{3,1,2,0:T(8,128)(2,1)}), s16[4,8,256,256]{3,1,2,0:T(8,128)(2,1)}, u32[]{:S(2)}, u32[]{:S(2)}) async-start(s16[4,8,256,256]{3,1,2,0:T(8,128)(2,1)} %pad_add_fusion), calls=%async_computation.1 | async-start | bytes 8388608 | tf_op jit(solution)/shard_map/all_to_all | solution.py:208
  118.0 124.9 %all-to-all-start = ((s16[32,256,256]{2,1,0:T(8,128)(2,1)}), s16[32,256,256]{2,1,0:T(8,128)(2,1)}, u32[]{:S(2)}, u32[]{:S(2)}) async-start(s16[32,256,256]{2,1,0:T(8,128)(2,1)} %copy.69), calls=%async_computation | async-start | bytes 8388608 | tf_op jit(solution)/shard_map/all_to_all | solution.py:217
  350.8 12.7 %copy-start.1 = (bf16[64,32]{1,0:T(8,128)(2,1)S(1)}, bf16[64,32]{1,0:T(8,128)(2,1)}, u32[]{:S(2)}) copy-start(bf16[64,32]{1,0:T(8,128)(2,1)} %constant.14.clone) | copy-start | bytes 12292
  350.8 12.7 %copy-start.4 = (bf16[64,32]{1,0:T(8,128)(2,1)S(1)}, bf16[64,32]{1,0:T(8,128)(2,1)}, u32[]{:S(2)}) copy-start(bf16[64,32]{1,0:T(8,128)(2,1)} %constant.13.clone) | copy-start | bytes 12292
  358.1 99.4 %all-to-all-start.2 = ((s16[8,256,1024]{1,0,2:T(8,128)(2,1)}), s16[8,256,1024]{1,0,2:T(8,128)(2,1)}, u32[]{:S(2)}, u32[]{:S(2)}) async-start(s16[8,256,1024]{1,0,2:T(8,128)(2,1)} %copy.76), calls=%async_computation.2 | async-start | bytes 8388608 | tf_op jit(solution)/shard_map/all_to_all | solution.py:226
  474.5 4.5 copy-start.8
  479.0 1.3 copy-start.7
  480.3 1.5 copy-start.10
  582.7 8.8 copy-start
  605.8 97.4 %all-to-all-start.3 = ((s16[32,256,256]{2,1,0:T(8,128)(2,1)}), s16[32,256,256]{2,1,0:T(8,128)(2,1)}, u32[]{:S(2)}, u32[]{:S(2)}) async-start(s16[32,256,256]{2,1,0:T(8,128)(2,1)} %copy.78), calls=%async_computation.3 | async-start | bytes 8388608 | tf_op jit(solution)/shard_map/all_to_all | solution.py:217
  610.9 4.3 slice-start
  613.9 2.2 slice-start.1
  703.2 97.9 %all-to-all-start.4 = ((s16[4,8,256,256]{3,1,2,0:T(8,128)(2,1)}), s16[4,8,256,256]{3,1,2,0:T(8,128)(2,1)}, u32[]{:S(2)}, u32[]{:S(2)}) async-start(s16[4,8,256,256]{3,1,2,0:T(8,128)(2,1)} %pad_add_fusion.1), calls=%async_computation.4 | async-start | bytes 8388608 | tf_op jit(solution)/shard_map/all_to_all | solution.py:208
  1176.3 2.2 copy-start.5
  1178.5 1.0 copy-start.6
  1179.5 1.5 copy-start.9
